TPU v7x, 32 devices: a whole 2x2x4 slice. The times are simulated.
32 devices in a mesh: row: 4 (over y, x), bus: 8 (over z, core).
Axes of the slice: x: 2, y: 2, z: 4, core: 2. Of those that a mesh axis runs over, the one named last changes fastest.
Arguments:
- monitored: bfloat16 [512, 32768], P('row', 'bus'), may hold values from -6 to 6
- outaged: bfloat16 [256, 32768], P('row', 'bus'), may hold values from -6 to 6
- bus_weight: float32 [32768], P('bus'), may hold values from 0.5 to 4
- lodf_table: float32 [1024], replicated, may hold values from -1.5 to 1.5
- mon_id: int32 [2048], P('row'), may hold values from 0 to 511
- out_id: int32 [2048], P('row'), may hold values from 0 to 255
- lodf_idx: int32 [2048], P('row'), may hold values from 0 to 1023
Outputs:
- gram: float32 [2048, 2048], P('row', 'bus')
All inputs are finite; a program needn't handle non-finite values.
Results may differ from a plain program's by a relative error of at most 0.0007.
Values may be sent and summed in bfloat16 or wider, within the bound.
A program may use at most 128 MiB of HBM per device.

v0:
```python
import functools

import jax
import jax.numpy as jnp
from jax import lax
from jax.experimental import pallas as pl
from jax.experimental.pallas import tpu as pltpu
from jax.sharding import PartitionSpec as P

BLK = 128
F32 = jnp.float32
BF16 = jnp.bfloat16
MESH = pl.DeviceIdType.MESH


def split(v):
    a = v.astype(BF16)
    return a, (v - a.astype(F32)).astype(BF16)


def dot(a, b):
    return jnp.dot(a, b, preferred_element_type=F32)


def dot_t(a, b):
    return lax.dot_general(a, b, (((1,), (1,)), ((), ())), preferred_element_type=F32)


def down(lanes):
    n = lanes.shape[1]
    return jnp.broadcast_to(lanes, (128, n)).T


def factors(idx, table_t, entries):
    n = idx.shape[1]
    parts = []
    for lo in range(0, n, 128):
        total = jnp.zeros((1, 128), F32)
        for e in range(0, entries, 128):
            rows = lax.broadcasted_iota(jnp.int32, (128, 128), 0) + e
            hit = jnp.where(rows == idx[:, lo:lo + 128], table_t[e:e + 128, :], 0.0)
            total = total + jnp.sum(hit, axis=0, keepdims=True)
        parts.append(total)
    return jnp.concatenate(parts, axis=1)


class Stream:
    def __init__(self, refs, blocks, me, core, other, axes):
        (self.gp, self.cbuf, self.acc, self.b1, self.s1, self.b2, self.full,
         self.cs, self.cr, self.p1s, self.p1r, self.p2s, self.p2r,
         self.a1s, self.a1r, self.a2s, self.a2r, self.ds, self.dr) = refs
        self.blocks = blocks
        self.core, self.other = core, other
        (self.n1, self.i1, self.dev1), (self.n2, self.i2, self.dev2) = axes
        self.H = self.gp.shape[0] // 2
        self.h1 = self.H // self.n1
        self.pz = self.h1 // self.n2
        self.z_first = me

    def compute(self, x, xw):
        at = 0
        for k in self.blocks:
            m = (k + 1) * BLK
            both = dot_t(x[:m, :], xw[k])
            self.gp[at:at + m, :] = both[:, :BLK] + both[:, BLK:]
            at += m
        if self.gp.shape[0] > at:
            self.gp[at:, :] = jnp.zeros((self.gp.shape[0] - at, BLK), F32)

    def rows(self, start, count):
        return pl.ds(pl.multiple_of(start, 8), count)

    def send(self, src, dst, s, r, dev):
        c = pltpu.make_async_remote_copy(
            src_ref=src, dst_ref=dst, send_sem=s, recv_sem=r, device_id=dev, device_id_type=MESH)
        c.start()
        return c

    def pair_start(self):
        self.c = [self.send(self.gp.at[self.rows((1 - self.core) * self.H, self.H), :], self.cbuf,
                            self.cs, self.cr, self.other)]

    def wait(self):
        for c in self.c:
            c.wait()

    def one_start(self):
        self.wait()
        self.acc[...] = self.gp[self.rows(self.core * self.H, self.H), :] + self.cbuf[...]
        self.c = []
        for d in range(1, self.n1):
            q = lax.rem(self.i1 + d, self.n1)
            self.c.append(self.send(self.acc.at[self.rows(q * self.h1, self.h1), :], self.b1.at[d - 1],
                                    self.p1s.at[d - 1], self.p1r.at[d - 1], self.dev1(q)))

    def two_start(self):
        self.wait()
        total = self.acc[self.rows(self.i1 * self.h1, self.h1), :]
        for d in range(1, self.n1):
            total = total + self.b1[d - 1]
        self.s1[...] = total
        self.c = []
        for d in range(1, self.n2):
            q = lax.rem(self.i2 + d, self.n2)
            self.c.append(self.send(self.s1.at[self.rows(q * self.pz, self.pz), :], self.b2.at[d - 1],
                                    self.p2s.at[d - 1], self.p2r.at[d - 1], self.dev2(q)))

    def piece(self, z, r):
        i1, i2 = (z, r) if self.z_first else (r, z)
        return self.rows(self.core * self.H + i1 * self.h1 + i2 * self.pz, self.pz)

    def back_start(self):
        self.wait()
        total = self.s1[self.rows(self.i2 * self.pz, self.pz), :]
        for d in range(1, self.n2):
            total = total + self.b2[d - 1]
        if self.z_first:
            self.Z, self.zi, self.zdev = self.n1, self.i1, self.dev1
            self.R, self.r, self.rdev = self.n2, self.i2, self.dev2
        else:
            self.Z, self.zi, self.zdev = self.n2, self.i2, self.dev2
            self.R, self.r, self.rdev = self.n1, self.i1, self.dev1
        at = self.piece(self.zi, self.r)
        self.full[at, :] = total
        ref = self.full.at[at, :]
        self.zc = []
        for d in range(1, self.Z):
            self.zc.append(self.send(ref, ref, self.a1s.at[d - 1], self.a1r.at[d - 1],
                                     self.zdev(lax.rem(self.zi + d, self.Z))))
        self.c = []
        self.spread(0)

    def spread(self, e):
        ref = self.full.at[self.piece(lax.rem(self.zi + self.Z - e, self.Z), self.r), :]
        for d in range(1, self.R):
            self.c.append(self.send(ref, ref, self.a2s.at[e, d - 1], self.a2r.at[e, d - 1],
                                    self.rdev(lax.rem(self.r + d, self.R))))

    def spread_rest(self):
        for e in range(1, self.Z):
            self.zc[e - 1].wait()
            self.spread(e)

    def pair_back(self):
        self.wait()
        ref = self.full.at[self.rows(self.core * self.H, self.H), :]
        self.c = [self.send(ref, ref, self.ds, self.dr, self.other)]


def select(ids, block, rows_each, dev_rows, axis, shape):
    p = lax.broadcasted_iota(jnp.int32, shape, axis)
    if axis == 1:
        p = p + block[1]
    shift = rows_each.bit_length() - 1
    line = lax.shift_right_logical(p, jnp.full(shape, shift, jnp.int32)) * (dev_rows - rows_each) + p
    return jnp.where(ids == line + block[0] * rows_each, 1.0, 0.0).astype(BF16)


def kernel(dims, mon_ref, out_ref, w_hbm, table_hbm, mid_hbm, oid_hbm, lid_hbm,
           gram_ref, w_ref, table_ref, mid_ref, oid_ref, lid_ref, small, x, xw, tt, ids, brow, t_o, t_m, x_s, x_r, i_s, i_r, own, own_i, *rest):
    R, B, nb_all = dims
    Z = B // 2
    r = lax.axis_index("row")
    b = lax.axis_index("bus")
    core = lax.rem(b, 2)
    zi = lax.div(b, 2)
    mrows, cols = mon_ref.shape
    orows = out_ref.shape[0]
    each = BLK // R
    cq = cols // R
    nblk_o, nblk_m = orows // each, mrows // each
    nblk = nblk_m + nblk_o
    kl = mid_ref.shape[1]
    kc = kl * R // B
    loads = []
    for i, (src, dst) in enumerate(((w_hbm, w_ref), (table_hbm, table_ref), (mid_hbm, mid_ref),
                                    (oid_hbm, oid_ref), (lid_hbm, lid_ref))):
        c = pltpu.make_async_copy(src, dst, small.at[i])
        c.start()
        loads.append(c)

    def row_dev(q):
        return {"row": q}

    def z_dev(q):
        return {"bus": q * 2 + core}

    pair_dev = {"bus": zi * 2 + (1 - core)}
    barrier = pltpu.get_barrier_semaphore()
    for d in range(1, R):
        pl.semaphore_signal(barrier, inc=1, device_id=row_dev(lax.rem(r + d, R)), device_id_type=MESH)
    for d in range(1, Z):
        pl.semaphore_signal(barrier, inc=1, device_id=z_dev(lax.rem(zi + d, Z)), device_id_type=MESH)
    pl.semaphore_signal(barrier, inc=1, device_id=pair_dev, device_id_type=MESH)
    pl.semaphore_wait(barrier, R - 1 + Z - 1 + 1)

    def source(k, q):
        ref, k = (out_ref, k) if k < nblk_o else (mon_ref, k - nblk_o)
        return ref.at[k * each:(k + 1) * each, pl.ds(pl.multiple_of(q * cq, 128), cq)]

    def target(k):
        return x.at[pl.ds(pl.multiple_of(k * BLK + r * each, each), each), :]

    chunks = []
    for k in range(nblk):
        chunk = []
        for d in range(1, R):
            q = lax.rem(r + d, R)
            c = pltpu.make_async_remote_copy(
                src_ref=source(k, q), dst_ref=target(k), send_sem=x_s.at[d - 1, k], recv_sem=x_r.at[d - 1, k],
                device_id=row_dev(q), device_id_type=MESH)
            c.start()
            chunk.append(c)
        c = pltpu.make_async_copy(source(k, r), target(k), own.at[k])
        c.start()
        chunk.append(c)
        chunks.append(chunk)
    for c in loads:
        c.wait()
    id_copies = []
    for i, src in enumerate((mid_ref, oid_ref, lid_ref)):
        for d in range(1, R):
            c = pltpu.make_async_remote_copy(
                src_ref=src, dst_ref=ids.at[i, r], send_sem=i_s.at[i, d - 1], recv_sem=i_r.at[i, d - 1],
                device_id=row_dev(lax.rem(r + d, R)), device_id_type=MESH)
            c.start()
            id_copies.append(c)
        c = pltpu.make_async_copy(src, ids.at[i, r], own_i.at[i])
        c.start()
        id_copies.append(c)

    entries = table_ref.shape[1]
    for e in range(0, entries, 128):
        tt[e:e + 128, :] = down(table_ref[:, e:e + 128])
    c_row = down(factors(lid_ref[...], tt, entries))
    oid_t = down(oid_ref[...].astype(F32)).astype(jnp.int32)
    mid_t = down(mid_ref[...].astype(F32)).astype(jnp.int32)
    for k in range(nblk):
        for e in range(0, BLK, 128):
            at = slice(k * BLK + e, k * BLK + e + 128)
            if k < nblk_o:
                brow[:, at] = select(oid_t, (k, e), each, orows, 1, (kl, 128))
            else:
                brow[:, at] = select(mid_t, (k - nblk_o, e), each, mrows, 1, (kl, 128))
    scale = w_ref[:, pl.ds(pl.multiple_of(r * cq, 128), cq)] * (1.0 / nb_all)

    z_axis, row_axis = (Z, zi, z_dev), (R, r, row_dev)
    n = len(rest) // 2
    s1, s2 = [
        Stream(rest[i * n:(i + 1) * n], blocks, z_first, core, pair_dev,
               (z_axis, row_axis) if z_first else (row_axis, z_axis))
        for i, (blocks, z_first) in enumerate(plan(nblk))]

    def arrive(k):
        for c in chunks[k]:
            c.wait()
        rows = slice(k * BLK, (k + 1) * BLK)
        v = x[rows, :].astype(F32) * scale
        h = v.astype(BF16)
        xw[k, :BLK, :] = h
        xw[k, BLK:, :] = (v - h.astype(F32)).astype(BF16)

    for stream in (s1, s2):
        for k in stream.blocks:
            arrive(k)
        stream.compute(x, xw)
        stream.pair_start()
        stream.one_start()
    s1.two_start()
    s2.two_start()
    s1.back_start()
    s2.back_start()
    s1.spread_rest()

    for c in id_copies:
        c.wait()
    owner = lax.div(b * kc, kl)
    begin = pl.multiple_of(lax.rem(b * kc, kl), 128)
    mid_c = ids[0, owner, :, pl.ds(begin, kc)]
    oid_c = ids[1, owner, :, pl.ds(begin, kc)]
    c_col = factors(ids[2, owner, :, pl.ds(begin, kc)], tt, entries)
    bcol = [select(oid_c, (k, 0), each, orows, 0, (BLK, kc)) for k in range(nblk_o)]
    bcol += [select(mid_c, (k, 0), each, mrows, 0, (BLK, kc)) for k in range(nblk_m)]

    t_o[...] = jnp.zeros_like(t_o)
    t_m[...] = jnp.zeros_like(t_m)
    cut = nblk_o * BLK

    def times(v, cols_of):
        total = None
        for p in split(v):
            total = dot(p, cols_of) if total is None else total + dot(p, cols_of)
        return total

    def gather(stream):
        stream.wait()
        at = 0
        for k in stream.blocks:
            m = (k + 1) * BLK
            strip = stream.full[at:at + m, :]
            at += m
            t = t_o if k < nblk_o else t_m
            t[:m, :] = t[:m, :] + times(strip, bcol[k])
            rows = slice(k * BLK, m)
            above = min(k * BLK, cut)
            if above > 0:
                part = jnp.concatenate(bcol[:above // BLK], axis=0)
                t_o[rows, :] = t_o[rows, :] + times(strip[:above, :].T, part)
            if k * BLK > cut:
                part = jnp.concatenate(bcol[nblk_o:k], axis=0)
                t_m[rows, :] = t_m[rows, :] + times(strip[cut:k * BLK, :].T, part)

    s2.spread_rest()
    s1.pair_back()
    gather(s1)
    s2.pair_back()
    gather(s2)
    t = t_m[...] + t_o[...] * c_col
    g_o = times_left(brow[:, :cut], t[:cut, :])
    g_m = times_left(brow[:, cut:], t[cut:, :])
    gram_ref[...] = g_m + g_o * jnp.concatenate([c_row] * (kc // 128), axis=1)


def times_left(s, v):
    a, b = split(v)
    return dot(s, a) + dot(s, b)


def plan(nblk):
    early = nblk - nblk // 3
    return (range(early), True), (range(early, nblk), False)


def solution(mesh):
    R, B = mesh.shape["row"], mesh.shape["bus"]
    Z = B // 2

    def stream_scratch(blocks, n1, n2):
        unit = 8 * R * B
        packed = -(-(blocks * BLK) // unit) * unit
        H = packed // 2
        h1 = H // n1
        pz = h1 // n2
        dma = pltpu.SemaphoreType.DMA
        return [
            pltpu.VMEM((packed, BLK), F32),
            pltpu.VMEM((H, BLK), F32),
            pltpu.VMEM((H, BLK), F32),
            pltpu.VMEM((n1 - 1, h1, BLK), F32),
            pltpu.VMEM((h1, BLK), F32),
            pltpu.VMEM((n2 - 1, pz, BLK), F32),
            pltpu.VMEM((packed, BLK), F32),
            dma, dma,
            dma((n1 - 1,)), dma((n1 - 1,)),
            dma((n2 - 1,)), dma((n2 - 1,)),
            dma((Z - 1,)), dma((Z - 1,)),
            dma((Z, R - 1)), dma((Z, R - 1)),
            dma, dma,
        ]

    def local(monitored, outaged, bus_weight, lodf_table, mon_id, out_id, lodf_idx):
        mrows, cols = monitored.shape
        orows = outaged.shape[0]
        n = (mrows + orows) * R
        cq = cols // R
        nblk = n // BLK
        kl = mon_id.shape[0]
        kc = kl * R // B
        vmem = pl.BlockSpec(memory_space=pltpu.VMEM)
        hbm = pl.BlockSpec(memory_space=pl.ANY)
        dma = pltpu.SemaphoreType.DMA
        return pl.pallas_call(
            functools.partial(kernel, (R, B, cols * B)),
            out_shape=jax.ShapeDtypeStruct((kl, kc), F32),
            in_specs=[hbm] * 7,
            out_specs=vmem,
            scratch_shapes=[
                pltpu.VMEM((1, cols), F32),
                pltpu.VMEM((1, lodf_table.shape[0]), F32),
                pltpu.VMEM((1, kl), jnp.int32),
                pltpu.VMEM((1, kl), jnp.int32),
                pltpu.VMEM((1, kl), jnp.int32),
                dma((5,)),
                pltpu.VMEM((n, cq), BF16),
                pltpu.VMEM((nblk, 2 * BLK, cq), BF16),
                pltpu.VMEM((lodf_table.shape[0], 128), F32),
                pltpu.VMEM((3, R, 1, kl), jnp.int32),
                pltpu.VMEM((kl, n), BF16),
                pltpu.VMEM((n, kc), F32),
                pltpu.VMEM((n, kc), F32),
                dma((R - 1, nblk)), dma((R - 1, nblk)),
                dma((3, R - 1)), dma((3, R - 1)),
                dma((nblk,)), dma((3,)),
            ] + [
                ref for blocks, z_first in plan(nblk)
                for ref in stream_scratch(sum(k + 1 for k in blocks), *((Z, R) if z_first else (R, Z)))
            ],
            compiler_params=pltpu.CompilerParams(
                collective_id=0, has_side_effects=True, vmem_limit_bytes=60 * 1024 * 1024),
        )(monitored, outaged, bus_weight[None, :], lodf_table[None, :],
          mon_id[None, :], out_id[None, :], lodf_idx[None, :])

    in_specs = (P("row", "bus"), P("row", "bus"), P("bus"), P(), P("row"), P("row"), P("row"))
    return jax.shard_map(local, mesh=mesh, in_specs=in_specs, out_specs=P("row", "bus"), check_vma=False)
```

profile of v0, /device:TPU:1, one launch (start us, length us, event | category | flops | bytes accessed | tf_op | source)
XLA Modules:
  0.0 53.6 jit_solution(4250015887655109313)
XLA Ops:
  0.0 51.7 %shard_map.73 = f32[512,256]{1,0:T(8,128)} custom-call(bf16[128,4096]{1,0:T(8,128)(2,1)} %mon_ref.1, bf16[64,4096]{1,0:T(8,128)(2,1)} %out_ref.1, f32[1,4096]{1,0:T(1,128)} %bitcast.5, f32[1,1024]{1,0:T(1,128)} %bitcast.6, s32[1,512]{1,0:T(1,128)} %bitcast.7, s32[1,512]{1,0:T(1,128)} %bitcast.8, s32[1,512]{1,0:T(1,128)} %bitcast.9), custom_call_target="tpu_custom_call" | custom-call | tf_op jit(solution)/shard_map/pallas_call | solution.py:372
  51.8 1.9 %copy.9 = f32[512,256]{1,0:T(8,128)} copy(f32[512,256]{1,0:T(8,128)} %shard_map.73) | data formatting | bytes 1048576
where the time goes:
time: 53.9 us; the launch traced here: 53.6 us
  Pallas kernels  51.7 us (96%)
  local copies, waits for them, and re-layouts  1.87 us (3%)
    pallas_call x1, Pallas kernels, local(): pl.pallas_call(functools.partial(kernel, (R, B, cols * B)), out_shape=jax...  51.7 us
    unnamed x1, local copies, waits for them, and re-layouts  1.87 us

commit v1 on v0

--- a/solution.py
+++ b/solution.py
@@ -8,8 +8,11 @@
 from jax.sharding import PartitionSpec as P
 
 BLK = 128
+BOUND = 6.0 * 6.0 * 4.0 * 1.01
 F32 = jnp.float32
 BF16 = jnp.bfloat16
+I16 = jnp.int16
+STAGED, DIRECT = 21, 14
 MESH = pl.DeviceIdType.MESH
 
 
@@ -24,6 +27,22 @@
 
 def dot_t(a, b):
     return lax.dot_general(a, b, (((1,), (1,)), ((), ())), preferred_element_type=F32)
+
+
+def encode(v, bound):
+    u = jnp.abs(v) * (1.0 / bound)
+    for _ in range(4):
+        u = jnp.sqrt(u)
+    u = jnp.minimum(u * 32767.0 + 0.5, 32767.0)
+    return jnp.where(v < 0, -u, u).astype(jnp.int32).astype(jnp.int16)
+
+
+def decode(q, bound):
+    f = q.astype(jnp.int32).astype(F32) * (bound ** (1 / 16) / 32767.0)
+    u = f
+    for _ in range(4):
+        u = u * u
+    return jnp.where(f < 0, -u, u)
 
 
 def down(lanes):
@@ -46,7 +65,7 @@
 
 class Stream:
     def __init__(self, refs, blocks, me, core, other, axes):
-        (self.gp, self.cbuf, self.acc, self.b1, self.s1, self.b2, self.full,
+        (self.gp, self.cbuf, self.acc, self.e1, self.b1, self.s1, self.e2, self.b2, self.full,
          self.cs, self.cr, self.p1s, self.p1r, self.p2s, self.p2r,
          self.a1s, self.a1r, self.a2s, self.a2r, self.ds, self.dr) = refs
         self.blocks = blocks
@@ -56,16 +75,13 @@
         self.h1 = self.H // self.n1
         self.pz = self.h1 // self.n2
         self.z_first = me
-
-    def compute(self, x, xw):
-        at = 0
-        for k in self.blocks:
-            m = (k + 1) * BLK
-            both = dot_t(x[:m, :], xw[k])
-            self.gp[at:at + m, :] = both[:, :BLK] + both[:, BLK:]
-            at += m
-        if self.gp.shape[0] > at:
-            self.gp[at:, :] = jnp.zeros((self.gp.shape[0] - at, BLK), F32)
+        self.at = 0
+
+    def strip(self, k, x, xw):
+        m = (k + 1) * BLK
+        both = dot_t(x[:m, :], xw[k])
+        self.gp[self.at:self.at + m, :] = both[:, :BLK] + both[:, BLK:]
+        self.at += m
 
     def rows(self, start, count):
         return pl.ds(pl.multiple_of(start, 8), count)
@@ -77,6 +93,8 @@
         return c
 
     def pair_start(self):
+        if self.gp.shape[0] > self.at:
+            self.gp[self.at:, :] = jnp.zeros((self.gp.shape[0] - self.at, BLK), F32)
         self.c = [self.send(self.gp.at[self.rows((1 - self.core) * self.H, self.H), :], self.cbuf,
                             self.cs, self.cr, self.other)]
 
@@ -86,43 +104,45 @@
 
     def one_start(self):
         self.wait()
-        self.acc[...] = self.gp[self.rows(self.core * self.H, self.H), :] + self.cbuf[...]
+        total = self.gp[self.rows(self.core * self.H, self.H), :] + self.cbuf[...]
+        self.acc[...] = total
+        self.e1[...] = encode(total, BOUND).reshape(self.e1.shape)
         self.c = []
         for d in range(1, self.n1):
             q = lax.rem(self.i1 + d, self.n1)
-            self.c.append(self.send(self.acc.at[self.rows(q * self.h1, self.h1), :], self.b1.at[d - 1],
+            self.c.append(self.send(self.e1.at[q], self.b1.at[d - 1],
                                     self.p1s.at[d - 1], self.p1r.at[d - 1], self.dev1(q)))
 
     def two_start(self):
         self.wait()
         total = self.acc[self.rows(self.i1 * self.h1, self.h1), :]
         for d in range(1, self.n1):
-            total = total + self.b1[d - 1]
+            total = total + decode(self.b1[d - 1], BOUND)
         self.s1[...] = total
+        self.e2[...] = encode(total, BOUND).reshape(self.e2.shape)
         self.c = []
         for d in range(1, self.n2):
             q = lax.rem(self.i2 + d, self.n2)
-            self.c.append(self.send(self.s1.at[self.rows(q * self.pz, self.pz), :], self.b2.at[d - 1],
+            self.c.append(self.send(self.e2.at[q], self.b2.at[d - 1],
                                     self.p2s.at[d - 1], self.p2r.at[d - 1], self.dev2(q)))
 
     def piece(self, z, r):
         i1, i2 = (z, r) if self.z_first else (r, z)
-        return self.rows(self.core * self.H + i1 * self.h1 + i2 * self.pz, self.pz)
+        return self.full.at[self.core, i1 * self.n2 + i2]
 
     def back_start(self):
         self.wait()
         total = self.s1[self.rows(self.i2 * self.pz, self.pz), :]
         for d in range(1, self.n2):
-            total = total + self.b2[d - 1]
+            total = total + decode(self.b2[d - 1], BOUND)
         if self.z_first:
             self.Z, self.zi, self.zdev = self.n1, self.i1, self.dev1
             self.R, self.r, self.rdev = self.n2, self.i2, self.dev2
         else:
             self.Z, self.zi, self.zdev = self.n2, self.i2, self.dev2
             self.R, self.r, self.rdev = self.n1, self.i1, self.dev1
-        at = self.piece(self.zi, self.r)
-        self.full[at, :] = total
-        ref = self.full.at[at, :]
+        ref = self.piece(self.zi, self.r)
+        ref[...] = encode(total, BOUND)
         self.zc = []
         for d in range(1, self.Z):
             self.zc.append(self.send(ref, ref, self.a1s.at[d - 1], self.a1r.at[d - 1],
@@ -131,7 +151,7 @@
         self.spread(0)
 
     def spread(self, e):
-        ref = self.full.at[self.piece(lax.rem(self.zi + self.Z - e, self.Z), self.r), :]
+        ref = self.piece(lax.rem(self.zi + self.Z - e, self.Z), self.r)
         for d in range(1, self.R):
             self.c.append(self.send(ref, ref, self.a2s.at[e, d - 1], self.a2r.at[e, d - 1],
                                     self.rdev(lax.rem(self.r + d, self.R))))
@@ -143,8 +163,44 @@
 
     def pair_back(self):
         self.wait()
-        ref = self.full.at[self.rows(self.core * self.H, self.H), :]
+        ref = self.full.at[self.core]
         self.c = [self.send(ref, ref, self.ds, self.dr, self.other)]
+
+
+class Direct(Stream):
+    def __init__(self, refs, blocks, core, other, axes):
+        (self.gp, self.cbuf, self.acc, self.e1, self.b1, self.full,
+         self.cs, self.cr, self.p1s, self.p1r, self.a1s, self.a1r, self.ds, self.dr) = refs
+        self.blocks = blocks
+        self.core, self.other = core, other
+        self.Z, self.zi, self.R, self.r = axes
+        self.H = self.gp.shape[0] // 2
+        self.pz = self.H // (self.Z * self.R)
+        self.at = 0
+
+    def peers(self):
+        for j in range(1, self.Z * self.R):
+            z = lax.rem(self.zi + j // self.R, self.Z)
+            r = lax.rem(self.r + j % self.R, self.R)
+            yield j - 1, z * self.R + r, {"row": r, "bus": z * 2 + self.core}
+
+    def one_start(self):
+        self.wait()
+        total = self.gp[self.rows(self.core * self.H, self.H), :] + self.cbuf[...]
+        self.acc[...] = total
+        self.e1[...] = encode(total, BOUND).reshape(self.e1.shape)
+        self.c = [self.send(self.e1.at[at], self.b1.at[j], self.p1s.at[j], self.p1r.at[j], dev)
+                  for j, at, dev in self.peers()]
+
+    def back_start(self):
+        self.wait()
+        me = self.zi * self.R + self.r
+        total = self.acc[self.rows(me * self.pz, self.pz), :]
+        for j in range(self.Z * self.R - 1):
+            total = total + decode(self.b1[j], BOUND)
+        ref = self.full.at[self.core, me]
+        ref[...] = encode(total, BOUND)
+        self.c = [self.send(ref, ref, self.a1s.at[j], self.a1r.at[j], dev) for j, _, dev in self.peers()]
 
 
 def select(ids, block, rows_each, dev_rows, axis, shape):
@@ -201,6 +257,18 @@
     def target(k):
         return x.at[pl.ds(pl.multiple_of(k * BLK + r * each, each), each), :]
 
+    id_copies = []
+    for i, src in enumerate((mid_hbm, oid_hbm, lid_hbm)):
+        for d in range(1, R):
+            c = pltpu.make_async_remote_copy(
+                src_ref=src, dst_ref=ids.at[i, r], send_sem=i_s.at[i, d - 1], recv_sem=i_r.at[i, d - 1],
+                device_id=row_dev(lax.rem(r + d, R)), device_id_type=MESH)
+            c.start()
+            id_copies.append(c)
+        c = pltpu.make_async_copy(src, ids.at[i, r], own_i.at[i])
+        c.start()
+        id_copies.append(c)
+
     chunks = []
     for k in range(nblk):
         chunk = []
@@ -217,17 +285,6 @@
         chunks.append(chunk)
     for c in loads:
         c.wait()
-    id_copies = []
-    for i, src in enumerate((mid_ref, oid_ref, lid_ref)):
-        for d in range(1, R):
-            c = pltpu.make_async_remote_copy(
-                src_ref=src, dst_ref=ids.at[i, r], send_sem=i_s.at[i, d - 1], recv_sem=i_r.at[i, d - 1],
-                device_id=row_dev(lax.rem(r + d, R)), device_id_type=MESH)
-            c.start()
-            id_copies.append(c)
-        c = pltpu.make_async_copy(src, ids.at[i, r], own_i.at[i])
-        c.start()
-        id_copies.append(c)
 
     entries = table_ref.shape[1]
     for e in range(0, entries, 128):
@@ -245,11 +302,13 @@
     scale = w_ref[:, pl.ds(pl.multiple_of(r * cq, 128), cq)] * (1.0 / nb_all)
 
     z_axis, row_axis = (Z, zi, z_dev), (R, r, row_dev)
-    n = len(rest) // 2
-    s1, s2 = [
-        Stream(rest[i * n:(i + 1) * n], blocks, z_first, core, pair_dev,
-               (z_axis, row_axis) if z_first else (row_axis, z_axis))
-        for i, (blocks, z_first) in enumerate(plan(nblk))]
+    streams, at = [], 0
+    for blocks, direct in plan(nblk):
+        n = DIRECT if direct else STAGED
+        refs = rest[at:at + n]
+        at += n
+        streams.append(Direct(refs, blocks, core, pair_dev, (Z, zi, R, r)) if direct else
+                       Stream(refs, blocks, True, core, pair_dev, (z_axis, row_axis)))
 
     def arrive(k):
         for c in chunks[k]:
@@ -260,17 +319,20 @@
         xw[k, :BLK, :] = h
         xw[k, BLK:, :] = (v - h.astype(F32)).astype(BF16)
 
-    for stream in (s1, s2):
+    def begin(stream):
         for k in stream.blocks:
             arrive(k)
-        stream.compute(x, xw)
+            stream.strip(k, x, xw)
         stream.pair_start()
         stream.one_start()
+
+    s1, s2, s3, s4 = streams
+    begin(s1)
+    begin(s2)
     s1.two_start()
+    begin(s3)
     s2.two_start()
-    s1.back_start()
-    s2.back_start()
-    s1.spread_rest()
+    begin(s4)
 
     for c in id_copies:
         c.wait()
@@ -295,9 +357,10 @@
     def gather(stream):
         stream.wait()
         at = 0
+        both = decode(stream.full[...], BOUND).reshape(stream.gp.shape)
         for k in stream.blocks:
             m = (k + 1) * BLK
-            strip = stream.full[at:at + m, :]
+            strip = both[at:at + m, :]
             at += m
             t = t_o if k < nblk_o else t_m
             t[:m, :] = t[:m, :] + times(strip, bcol[k])
@@ -310,11 +373,20 @@
                 part = jnp.concatenate(bcol[nblk_o:k], axis=0)
                 t_m[rows, :] = t_m[rows, :] + times(strip[cut:k * BLK, :].T, part)
 
+    s1.back_start()
+    s2.back_start()
+    s3.back_start()
+    s4.back_start()
+    s1.spread_rest()
     s2.spread_rest()
+    s3.pair_back()
     s1.pair_back()
+    s2.pair_back()
+    gather(s3)
+    s4.pair_back()
     gather(s1)
-    s2.pair_back()
     gather(s2)
+    gather(s4)
     t = t_m[...] + t_o[...] * c_col
     g_o = times_left(brow[:, :cut], t[:cut, :])
     g_m = times_left(brow[:, cut:], t[cut:, :])
@@ -327,8 +399,8 @@
 
 
 def plan(nblk):
-    early = nblk - nblk // 3
-    return (range(early), True), (range(early, nblk), False)
+    cuts = [0, nblk // 2, nblk - 2, nblk - 1, nblk]
+    return [(range(a, b), i > 1) for i, (a, b) in enumerate(zip(cuts, cuts[1:]))]
 
 
 def solution(mesh):
@@ -346,15 +418,36 @@
             pltpu.VMEM((packed, BLK), F32),
             pltpu.VMEM((H, BLK), F32),
             pltpu.VMEM((H, BLK), F32),
-            pltpu.VMEM((n1 - 1, h1, BLK), F32),
+            pltpu.VMEM((n1, h1, BLK), I16),
+            pltpu.VMEM((n1 - 1, h1, BLK), I16),
             pltpu.VMEM((h1, BLK), F32),
-            pltpu.VMEM((n2 - 1, pz, BLK), F32),
-            pltpu.VMEM((packed, BLK), F32),
+            pltpu.VMEM((n2, pz, BLK), I16),
+            pltpu.VMEM((n2 - 1, pz, BLK), I16),
+            pltpu.VMEM((2, n1 * n2, pz, BLK), I16),
             dma, dma,
             dma((n1 - 1,)), dma((n1 - 1,)),
             dma((n2 - 1,)), dma((n2 - 1,)),
             dma((Z - 1,)), dma((Z - 1,)),
             dma((Z, R - 1)), dma((Z, R - 1)),
+            dma, dma,
+        ]
+
+    def direct_scratch(blocks):
+        unit = 8 * R * B
+        packed = -(-(blocks * BLK) // unit) * unit
+        H = packed // 2
+        n = R * Z
+        dma = pltpu.SemaphoreType.DMA
+        return [
+            pltpu.VMEM((packed, BLK), F32),
+            pltpu.VMEM((H, BLK), F32),
+            pltpu.VMEM((H, BLK), F32),
+            pltpu.VMEM((n, H // n, BLK), I16),
+            pltpu.VMEM((n - 1, H // n, BLK), I16),
+            pltpu.VMEM((2, n, H // n, BLK), I16),
+            dma, dma,
+            dma((n - 1,)), dma((n - 1,)),
+            dma((n - 1,)), dma((n - 1,)),
             dma, dma,
         ]
 
@@ -369,6 +462,7 @@
         vmem = pl.BlockSpec(memory_space=pltpu.VMEM)
         hbm = pl.BlockSpec(memory_space=pl.ANY)
         dma = pltpu.SemaphoreType.DMA
+        streams = plan(nblk)
         return pl.pallas_call(
             functools.partial(kernel, (R, B, cols * B)),
             out_shape=jax.ShapeDtypeStruct((kl, kc), F32),
@@ -392,8 +486,9 @@
                 dma((3, R - 1)), dma((3, R - 1)),
                 dma((nblk,)), dma((3,)),
             ] + [
-                ref for blocks, z_first in plan(nblk)
-                for ref in stream_scratch(sum(k + 1 for k in blocks), *((Z, R) if z_first else (R, Z)))
+                ref for blocks, direct in streams
+                for ref in (direct_scratch(sum(k + 1 for k in blocks)) if direct else
+                            stream_scratch(sum(k + 1 for k in blocks), Z, R))
             ],
             compiler_params=pltpu.CompilerParams(
                 collective_id=0, has_side_effects=True, vmem_limit_bytes=60 * 1024 * 1024),

time: 53.9 us -> 46.7 us (0.87)
  Pallas kernels: 51.7 us -> 44.6 us
    pallas_call x1, Pallas kernels: 51.7 us -> 44.6 us  [local(): pl.pallas_call(functools.partial(kernel, (R, B, cols * B)), out_shape=jax...]
where the time goes in v1:
time: 46.7 us; the launch traced here: 46.5 us
  Pallas kernels  44.6 us (96%)
  local copies, waits for them, and re-layouts  1.87 us (4%)
    pallas_call x1, Pallas kernels, local(): pl.pallas_call(functools.partial(kernel, (R, B, cols * B)), out_shape=jax...  44.6 us
    unnamed x1, local copies, waits for them, and re-layouts  1.87 us

profile of v1, /device:TPU:1, one launch (start us, length us, event | category | flops | bytes accessed | tf_op | source)
XLA Modules:
  0.0 46.5 jit_solution(14329286203210039898)
XLA Ops:
  0.0 44.6 %shard_map.73 = f32[512,256]{1,0:T(8,128)} custom-call(bf16[128,4096]{1,0:T(8,128)(2,1)} %mon_ref.1, bf16[64,4096]{1,0:T(8,128)(2,1)} %out_ref.1, f32[1,4096]{1,0:T(1,128)} %bitcast.5, f32[1,1024]{1,0:T(1,128)} %bitcast.6, s32[1,512]{1,0:T(1,128)} %bitcast.7, s32[1,512]{1,0:T(1,128)} %bitcast.8, s32[1,512]{1,0:T(1,128)} %bitcast.9), custom_call_target="tpu_custom_call" | custom-call | tf_op jit(solution)/shard_map/pallas_call | solution.py:466
  44.6 1.9 %copy.9 = f32[512,256]{1,0:T(8,128)} copy(f32[512,256]{1,0:T(8,128)} %shard_map.73) | data formatting | bytes 1048576

commit v2 on v1

--- a/solution.py
+++ b/solution.py
@@ -12,7 +12,7 @@
 F32 = jnp.float32
 BF16 = jnp.bfloat16
 I16 = jnp.int16
-STAGED, DIRECT = 21, 14
+STAGED, DIRECT = 11, 8
 MESH = pl.DeviceIdType.MESH
 
 
@@ -63,18 +63,20 @@
     return jnp.concatenate(parts, axis=1)
 
 
+def arrived(ref, sem):
+    pltpu.make_async_copy(ref, ref, sem).wait()
+
+
+def send(src, dst, s, r, dev):
+    pltpu.make_async_remote_copy(
+        src_ref=src, dst_ref=dst, send_sem=s, recv_sem=r, device_id=dev, device_id_type=MESH).start()
+
+
 class Stream:
-    def __init__(self, refs, blocks, me, core, other, axes):
-        (self.gp, self.cbuf, self.acc, self.e1, self.b1, self.s1, self.e2, self.b2, self.full,
-         self.cs, self.cr, self.p1s, self.p1r, self.p2s, self.p2r,
-         self.a1s, self.a1r, self.a2s, self.a2r, self.ds, self.dr) = refs
+    def setup(self, blocks, core, other):
         self.blocks = blocks
         self.core, self.other = core, other
-        (self.n1, self.i1, self.dev1), (self.n2, self.i2, self.dev2) = axes
         self.H = self.gp.shape[0] // 2
-        self.h1 = self.H // self.n1
-        self.pz = self.h1 // self.n2
-        self.z_first = me
         self.at = 0
 
     def strip(self, k, x, xw):
@@ -86,121 +88,134 @@
     def rows(self, start, count):
         return pl.ds(pl.multiple_of(start, 8), count)
 
-    def send(self, src, dst, s, r, dev):
-        c = pltpu.make_async_remote_copy(
-            src_ref=src, dst_ref=dst, send_sem=s, recv_sem=r, device_id=dev, device_id_type=MESH)
-        c.start()
-        return c
+    def half(self, core):
+        return self.gp.at[self.rows(core * self.H, self.H), :]
 
     def pair_start(self):
         if self.gp.shape[0] > self.at:
             self.gp[self.at:, :] = jnp.zeros((self.gp.shape[0] - self.at, BLK), F32)
-        self.c = [self.send(self.gp.at[self.rows((1 - self.core) * self.H, self.H), :], self.cbuf,
-                            self.cs, self.cr, self.other)]
-
-    def wait(self):
-        for c in self.c:
-            c.wait()
-
-    def one_start(self):
-        self.wait()
-        total = self.gp[self.rows(self.core * self.H, self.H), :] + self.cbuf[...]
+        send(self.half(1 - self.core), self.cbuf, self.cs, self.cr, self.other)
+
+    def pair_sum(self):
+        arrived(self.cbuf, self.cr)
+        total = self.half(self.core)[...] + self.cbuf[...]
         self.acc[...] = total
         self.e1[...] = encode(total, BOUND).reshape(self.e1.shape)
-        self.c = []
-        for d in range(1, self.n1):
-            q = lax.rem(self.i1 + d, self.n1)
-            self.c.append(self.send(self.e1.at[q], self.b1.at[d - 1],
-                                    self.p1s.at[d - 1], self.p1r.at[d - 1], self.dev1(q)))
+
+    def pair_back(self):
+        ref = self.full.at[self.core]
+        send(ref, ref, self.ds, self.dr, self.other)
+
+    def whole(self):
+        arrived(self.full.at[1 - self.core], self.dr)
+        return decode(self.full[...], BOUND).reshape(self.gp.shape)
+
+
+class Staged(Stream):
+    def __init__(self, refs, blocks, core, other, axes):
+        (self.gp, self.cbuf, self.acc, self.e1, self.b1, self.s1, self.e2, self.b2, self.full, sem, self.zr) = refs
+        (self.cs, self.cr, self.p1s, self.p1r, self.p2s, self.p2r,
+         self.a1s, self.a2s, self.a2r, self.ds, self.dr) = [sem.at[i] for i in range(STAGED)]
+        self.setup(blocks, core, other)
+        (self.Z, self.zi, self.zdev), (self.R, self.r, self.rdev) = axes
+        self.h1 = self.H // self.Z
+        self.pz = self.h1 // self.R
+
+    def one_start(self):
+        self.pair_sum()
+        for d in range(1, self.Z):
+            q = lax.rem(self.zi + d, self.Z)
+            send(self.e1.at[q], self.b1.at[d - 1], self.p1s, self.p1r, self.zdev(q))
 
     def two_start(self):
-        self.wait()
-        total = self.acc[self.rows(self.i1 * self.h1, self.h1), :]
-        for d in range(1, self.n1):
+        arrived(self.b1, self.p1r)
+        total = self.acc[self.rows(self.zi * self.h1, self.h1), :]
+        for d in range(1, self.Z):
             total = total + decode(self.b1[d - 1], BOUND)
         self.s1[...] = total
         self.e2[...] = encode(total, BOUND).reshape(self.e2.shape)
-        self.c = []
-        for d in range(1, self.n2):
-            q = lax.rem(self.i2 + d, self.n2)
-            self.c.append(self.send(self.e2.at[q], self.b2.at[d - 1],
-                                    self.p2s.at[d - 1], self.p2r.at[d - 1], self.dev2(q)))
-
-    def piece(self, z, r):
-        i1, i2 = (z, r) if self.z_first else (r, z)
-        return self.full.at[self.core, i1 * self.n2 + i2]
+        for d in range(1, self.R):
+            q = lax.rem(self.r + d, self.R)
+            send(self.e2.at[q], self.b2.at[d - 1], self.p2s, self.p2r, self.rdev(q))
+
+    def piece(self, z):
+        return self.full.at[self.core, z * self.R + self.r]
 
     def back_start(self):
-        self.wait()
-        total = self.s1[self.rows(self.i2 * self.pz, self.pz), :]
-        for d in range(1, self.n2):
+        arrived(self.b2, self.p2r)
+        total = self.s1[self.rows(self.r * self.pz, self.pz), :]
+        for d in range(1, self.R):
             total = total + decode(self.b2[d - 1], BOUND)
-        if self.z_first:
-            self.Z, self.zi, self.zdev = self.n1, self.i1, self.dev1
-            self.R, self.r, self.rdev = self.n2, self.i2, self.dev2
-        else:
-            self.Z, self.zi, self.zdev = self.n2, self.i2, self.dev2
-            self.R, self.r, self.rdev = self.n1, self.i1, self.dev1
-        ref = self.piece(self.zi, self.r)
+        ref = self.piece(self.zi)
         ref[...] = encode(total, BOUND)
-        self.zc = []
         for d in range(1, self.Z):
-            self.zc.append(self.send(ref, ref, self.a1s.at[d - 1], self.a1r.at[d - 1],
-                                     self.zdev(lax.rem(self.zi + d, self.Z))))
-        self.c = []
-        self.spread(0)
-
-    def spread(self, e):
-        ref = self.piece(lax.rem(self.zi + self.Z - e, self.Z), self.r)
+            send(ref, ref, self.a1s, self.zr.at[d - 1], self.zdev(lax.rem(self.zi + d, self.Z)))
+        self.spread(ref)
+
+    def spread(self, ref):
         for d in range(1, self.R):
-            self.c.append(self.send(ref, ref, self.a2s.at[e, d - 1], self.a2r.at[e, d - 1],
-                                    self.rdev(lax.rem(self.r + d, self.R))))
+            send(ref, ref, self.a2s, self.a2r, self.rdev(lax.rem(self.r + d, self.R)))
 
     def spread_rest(self):
         for e in range(1, self.Z):
-            self.zc[e - 1].wait()
-            self.spread(e)
+            ref = self.piece(lax.rem(self.zi + self.Z - e, self.Z))
+            arrived(ref, self.zr.at[e - 1])
+            self.spread(ref)
 
     def pair_back(self):
-        self.wait()
-        ref = self.full.at[self.core]
-        self.c = [self.send(ref, ref, self.ds, self.dr, self.other)]
+        arrived(self.full.at[self.core, :self.Z * (self.R - 1)], self.a2r)
+        super().pair_back()
+
+    def finish(self):
+        arrived(self.cbuf, self.cs)
+        arrived(self.b1, self.p1s)
+        arrived(self.b2, self.p2s)
+        arrived(self.full.at[0, :self.Z - 1], self.a1s)
+        arrived(self.full.at[0, :self.Z * (self.R - 1)], self.a2s)
+        arrived(self.full.at[0], self.ds)
 
 
 class Direct(Stream):
     def __init__(self, refs, blocks, core, other, axes):
-        (self.gp, self.cbuf, self.acc, self.e1, self.b1, self.full,
-         self.cs, self.cr, self.p1s, self.p1r, self.a1s, self.a1r, self.ds, self.dr) = refs
-        self.blocks = blocks
-        self.core, self.other = core, other
-        self.Z, self.zi, self.R, self.r = axes
-        self.H = self.gp.shape[0] // 2
-        self.pz = self.H // (self.Z * self.R)
-        self.at = 0
+        self.gp, self.cbuf, self.acc, self.e1, self.b1, self.full, sem = refs
+        (self.cs, self.cr, self.p1s, self.p1r, self.a1s, self.a1r, self.ds, self.dr) = [
+            sem.at[i] for i in range(DIRECT)]
+        self.setup(blocks, core, other)
+        (self.Z, self.zi, _), (self.R, self.r, _) = axes
+        self.N = self.Z * self.R
+        self.pz = self.H // self.N
 
     def peers(self):
-        for j in range(1, self.Z * self.R):
+        for j in range(1, self.N):
             z = lax.rem(self.zi + j // self.R, self.Z)
             r = lax.rem(self.r + j % self.R, self.R)
             yield j - 1, z * self.R + r, {"row": r, "bus": z * 2 + self.core}
 
     def one_start(self):
-        self.wait()
-        total = self.gp[self.rows(self.core * self.H, self.H), :] + self.cbuf[...]
-        self.acc[...] = total
-        self.e1[...] = encode(total, BOUND).reshape(self.e1.shape)
-        self.c = [self.send(self.e1.at[at], self.b1.at[j], self.p1s.at[j], self.p1r.at[j], dev)
-                  for j, at, dev in self.peers()]
+        self.pair_sum()
+        for j, at, dev in self.peers():
+            send(self.e1.at[at], self.b1.at[j], self.p1s, self.p1r, dev)
 
     def back_start(self):
-        self.wait()
+        arrived(self.b1, self.p1r)
         me = self.zi * self.R + self.r
         total = self.acc[self.rows(me * self.pz, self.pz), :]
-        for j in range(self.Z * self.R - 1):
+        for j in range(self.N - 1):
             total = total + decode(self.b1[j], BOUND)
         ref = self.full.at[self.core, me]
         ref[...] = encode(total, BOUND)
-        self.c = [self.send(ref, ref, self.a1s.at[j], self.a1r.at[j], dev) for j, _, dev in self.peers()]
+        for _, _, dev in self.peers():
+            send(ref, ref, self.a1s, self.a1r, dev)
+
+    def pair_back(self):
+        arrived(self.full.at[self.core, :self.N - 1], self.a1r)
+        super().pair_back()
+
+    def finish(self):
+        arrived(self.cbuf, self.cs)
+        arrived(self.b1, self.p1s)
+        arrived(self.full.at[0, :self.N - 1], self.a1s)
+        arrived(self.full.at[0], self.ds)
 
 
 def select(ids, block, rows_each, dev_rows, axis, shape):
@@ -213,7 +228,7 @@
 
 
 def kernel(dims, mon_ref, out_ref, w_hbm, table_hbm, mid_hbm, oid_hbm, lid_hbm,
-           gram_ref, w_ref, table_ref, mid_ref, oid_ref, lid_ref, small, x, xw, tt, ids, brow, t_o, t_m, x_s, x_r, i_s, i_r, own, own_i, *rest):
+           gram_ref, w_ref, table_ref, mid_ref, oid_ref, lid_ref, small, x, xw, tt, ids, brow, t_o, t_m, x_s, x_r, i_s, i_r, *rest):
     R, B, nb_all = dims
     Z = B // 2
     r = lax.axis_index("row")
@@ -226,6 +241,7 @@
     cq = cols // R
     nblk_o, nblk_m = orows // each, mrows // each
     nblk = nblk_m + nblk_o
+    n_sent = (R - 1) * (mrows + orows)
     kl = mid_ref.shape[1]
     kc = kl * R // B
     loads = []
@@ -257,32 +273,16 @@
     def target(k):
         return x.at[pl.ds(pl.multiple_of(k * BLK + r * each, each), each), :]
 
-    id_copies = []
     for i, src in enumerate((mid_hbm, oid_hbm, lid_hbm)):
         for d in range(1, R):
-            c = pltpu.make_async_remote_copy(
-                src_ref=src, dst_ref=ids.at[i, r], send_sem=i_s.at[i, d - 1], recv_sem=i_r.at[i, d - 1],
-                device_id=row_dev(lax.rem(r + d, R)), device_id_type=MESH)
-            c.start()
-            id_copies.append(c)
-        c = pltpu.make_async_copy(src, ids.at[i, r], own_i.at[i])
-        c.start()
-        id_copies.append(c)
-
-    chunks = []
+            send(src, ids.at[i, r], i_s, i_r, row_dev(lax.rem(r + d, R)))
+        pltpu.make_async_copy(src, ids.at[i, r], i_r).start()
+
     for k in range(nblk):
-        chunk = []
         for d in range(1, R):
             q = lax.rem(r + d, R)
-            c = pltpu.make_async_remote_copy(
-                src_ref=source(k, q), dst_ref=target(k), send_sem=x_s.at[d - 1, k], recv_sem=x_r.at[d - 1, k],
-                device_id=row_dev(q), device_id_type=MESH)
-            c.start()
-            chunk.append(c)
-        c = pltpu.make_async_copy(source(k, r), target(k), own.at[k])
-        c.start()
-        chunk.append(c)
-        chunks.append(chunk)
+            send(source(k, q), target(k), x_s, x_r.at[k], row_dev(q))
+        pltpu.make_async_copy(source(k, r), target(k), x_r.at[k]).start()
     for c in loads:
         c.wait()
 
@@ -304,16 +304,13 @@
     z_axis, row_axis = (Z, zi, z_dev), (R, r, row_dev)
     streams, at = [], 0
     for blocks, direct in plan(nblk):
-        n = DIRECT if direct else STAGED
-        refs = rest[at:at + n]
+        kind, n = (Direct, 7) if direct else (Staged, 11)
+        streams.append(kind(rest[at:at + n], blocks, core, pair_dev, (z_axis, row_axis)))
         at += n
-        streams.append(Direct(refs, blocks, core, pair_dev, (Z, zi, R, r)) if direct else
-                       Stream(refs, blocks, True, core, pair_dev, (z_axis, row_axis)))
 
     def arrive(k):
-        for c in chunks[k]:
-            c.wait()
         rows = slice(k * BLK, (k + 1) * BLK)
+        arrived(x.at[rows, :], x_r.at[k])
         v = x[rows, :].astype(F32) * scale
         h = v.astype(BF16)
         xw[k, :BLK, :] = h
@@ -334,8 +331,7 @@
     s2.two_start()
     begin(s4)
 
-    for c in id_copies:
-        c.wait()
+    arrived(ids, i_r)
     owner = lax.div(b * kc, kl)
     begin = pl.multiple_of(lax.rem(b * kc, kl), 128)
     mid_c = ids[0, owner, :, pl.ds(begin, kc)]
@@ -355,9 +351,8 @@
         return total
 
     def gather(stream):
-        stream.wait()
         at = 0
-        both = decode(stream.full[...], BOUND).reshape(stream.gp.shape)
+        both = stream.whole()
         for k in stream.blocks:
             m = (k + 1) * BLK
             strip = both[at:at + m, :]
@@ -391,6 +386,10 @@
     g_o = times_left(brow[:, :cut], t[:cut, :])
     g_m = times_left(brow[:, cut:], t[cut:, :])
     gram_ref[...] = g_m + g_o * jnp.concatenate([c_row] * (kc // 128), axis=1)
+    arrived(x.at[:n_sent, :], x_s)
+    arrived(ids.at[:, :R - 1], i_s)
+    for stream in streams:
+        stream.finish()
 
 
 def times_left(s, v):
@@ -424,12 +423,7 @@
             pltpu.VMEM((n2, pz, BLK), I16),
             pltpu.VMEM((n2 - 1, pz, BLK), I16),
             pltpu.VMEM((2, n1 * n2, pz, BLK), I16),
-            dma, dma,
-            dma((n1 - 1,)), dma((n1 - 1,)),
-            dma((n2 - 1,)), dma((n2 - 1,)),
-            dma((Z - 1,)), dma((Z - 1,)),
-            dma((Z, R - 1)), dma((Z, R - 1)),
-            dma, dma,
+            dma((STAGED,)), dma((Z - 1,)),
         ]
 
     def direct_scratch(blocks):
@@ -445,10 +439,7 @@
             pltpu.VMEM((n, H // n, BLK), I16),
             pltpu.VMEM((n - 1, H // n, BLK), I16),
             pltpu.VMEM((2, n, H // n, BLK), I16),
-            dma, dma,
-            dma((n - 1,)), dma((n - 1,)),
-            dma((n - 1,)), dma((n - 1,)),
-            dma, dma,
+            dma((DIRECT,)),
         ]
 
     def local(monitored, outaged, bus_weight, lodf_table, mon_id, out_id, lodf_idx):
@@ -482,9 +473,7 @@
                 pltpu.VMEM((kl, n), BF16),
                 pltpu.VMEM((n, kc), F32),
                 pltpu.VMEM((n, kc), F32),
-                dma((R - 1, nblk)), dma((R - 1, nblk)),
-                dma((3, R - 1)), dma((3, R - 1)),
-                dma((nblk,)), dma((3,)),
+                dma, dma((nblk,)), dma, dma,
             ] + [
                 ref for blocks, direct in streams
                 for ref in (direct_scratch(sum(k + 1 for k in blocks)) if direct else

time: 46.7 us -> 43.8 us (0.938)
  Pallas kernels: 44.6 us -> 41.8 us
    pallas_call x1, Pallas kernels: 44.6 us -> 41.8 us  [local(): pl.pallas_call(functools.partial(kernel, (R, B, cols * B)), out_shape=jax...]
where the time goes in v2:
time: 43.8 us; the launch traced here: 43.6 us
  Pallas kernels  41.8 us (95%)
  local copies, waits for them, and re-layouts  1.87 us (4%)
    pallas_call x1, Pallas kernels, local(): pl.pallas_call(functools.partial(kernel, (R, B, cols * B)), out_shape=jax...  41.8 us
    unnamed x1, local copies, waits for them, and re-layouts  1.87 us

profile of v2, /device:TPU:1, one launch (start us, length us, event | category | flops | bytes accessed | tf_op | source)
XLA Modules:
  0.0 43.6 jit_solution(15118702399578519323)
XLA Ops:
  0.0 41.8 %shard_map.73 = f32[512,256]{1,0:T(8,128)} custom-call(bf16[128,4096]{1,0:T(8,128)(2,1)} %mon_ref.1, bf16[64,4096]{1,0:T(8,128)(2,1)} %out_ref.1, f32[1,4096]{1,0:T(1,128)} %bitcast.5, f32[1,1024]{1,0:T(1,128)} %bitcast.6, s32[1,512]{1,0:T(1,128)} %bitcast.7, s32[1,512]{1,0:T(1,128)} %bitcast.8, s32[1,512]{1,0:T(1,128)} %bitcast.9), custom_call_target="tpu_custom_call" | custom-call | tf_op jit(solution)/shard_map/pallas_call | solution.py:457
  41.8 1.9 %copy.9 = f32[512,256]{1,0:T(8,128)} copy(f32[512,256]{1,0:T(8,128)} %shard_map.73) | data formatting | bytes 1048576

commit v3 on v2

--- a/solution.py
+++ b/solution.py
@@ -85,6 +85,11 @@
         self.gp[self.at:self.at + m, :] = both[:, :BLK] + both[:, BLK:]
         self.at += m
 
+    def strip_half(self, k, x, xw, core):
+        rows = pl.ds(pl.multiple_of(core * self.H, BLK), self.H)
+        both = dot_t(x[rows, :], xw[k])
+        self.gp[rows, :] = both[:, :BLK] + both[:, BLK:]
+
     def rows(self, start, count):
         return pl.ds(pl.multiple_of(start, 8), count)
 
@@ -166,10 +171,12 @@
         arrived(self.full.at[self.core, :self.Z * (self.R - 1)], self.a2r)
         super().pair_back()
 
-    def finish(self):
+    def settle(self):
         arrived(self.cbuf, self.cs)
         arrived(self.b1, self.p1s)
         arrived(self.b2, self.p2s)
+
+    def finish(self):
         arrived(self.full.at[0, :self.Z - 1], self.a1s)
         arrived(self.full.at[0, :self.Z * (self.R - 1)], self.a2s)
         arrived(self.full.at[0], self.ds)
@@ -186,7 +193,7 @@
         self.pz = self.H // self.N
 
     def peers(self):
-        for j in range(1, self.N):
+        for j in sorted(range(1, self.N), key=lambda j: (-min(j // self.R, self.Z - j // self.R), -(j % self.R))):
             z = lax.rem(self.zi + j // self.R, self.Z)
             r = lax.rem(self.r + j % self.R, self.R)
             yield j - 1, z * self.R + r, {"row": r, "bus": z * 2 + self.core}
@@ -211,9 +218,11 @@
         arrived(self.full.at[self.core, :self.N - 1], self.a1r)
         super().pair_back()
 
-    def finish(self):
+    def settle(self):
         arrived(self.cbuf, self.cs)
         arrived(self.b1, self.p1s)
+
+    def finish(self):
         arrived(self.full.at[0, :self.N - 1], self.a1s)
         arrived(self.full.at[0], self.ds)
 
@@ -228,7 +237,7 @@
 
 
 def kernel(dims, mon_ref, out_ref, w_hbm, table_hbm, mid_hbm, oid_hbm, lid_hbm,
-           gram_ref, w_ref, table_ref, mid_ref, oid_ref, lid_ref, small, x, xw, tt, ids, brow, t_o, t_m, x_s, x_r, i_s, i_r, *rest):
+           gram_ref, w_ref, table_ref, mid_ref, oid_ref, lid_ref, small, x, xw, tt, ids, brow, t_o, t_m, x_s, x_r, i_s, i_r, gram, g_s, *rest):
     R, B, nb_all = dims
     Z = B // 2
     r = lax.axis_index("row")
@@ -244,13 +253,6 @@
     n_sent = (R - 1) * (mrows + orows)
     kl = mid_ref.shape[1]
     kc = kl * R // B
-    loads = []
-    for i, (src, dst) in enumerate(((w_hbm, w_ref), (table_hbm, table_ref), (mid_hbm, mid_ref),
-                                    (oid_hbm, oid_ref), (lid_hbm, lid_ref))):
-        c = pltpu.make_async_copy(src, dst, small.at[i])
-        c.start()
-        loads.append(c)
-
     def row_dev(q):
         return {"row": q}
 
@@ -264,6 +266,12 @@
     for d in range(1, Z):
         pl.semaphore_signal(barrier, inc=1, device_id=z_dev(lax.rem(zi + d, Z)), device_id_type=MESH)
     pl.semaphore_signal(barrier, inc=1, device_id=pair_dev, device_id_type=MESH)
+    loads = []
+    for i, (src, dst) in enumerate(((w_hbm, w_ref), (table_hbm, table_ref), (mid_hbm, mid_ref),
+                                    (oid_hbm, oid_ref), (lid_hbm, lid_ref))):
+        c = pltpu.make_async_copy(src, dst, small.at[i])
+        c.start()
+        loads.append(c)
     pl.semaphore_wait(barrier, R - 1 + Z - 1 + 1)
 
     def source(k, q):
@@ -273,16 +281,19 @@
     def target(k):
         return x.at[pl.ds(pl.multiple_of(k * BLK + r * each, each), each), :]
 
-    for i, src in enumerate((mid_hbm, oid_hbm, lid_hbm)):
-        for d in range(1, R):
-            send(src, ids.at[i, r], i_s, i_r, row_dev(lax.rem(r + d, R)))
-        pltpu.make_async_copy(src, ids.at[i, r], i_r).start()
+    def send_ids():
+        for i, src in enumerate((mid_hbm, oid_hbm, lid_hbm)):
+            for d in range(1, R):
+                send(src, ids.at[i, r], i_s, i_r, row_dev(lax.rem(r + d, R)))
+            pltpu.make_async_copy(src, ids.at[i, r], i_r).start()
 
     for k in range(nblk):
         for d in range(1, R):
             q = lax.rem(r + d, R)
             send(source(k, q), target(k), x_s, x_r.at[k], row_dev(q))
         pltpu.make_async_copy(source(k, r), target(k), x_r.at[k]).start()
+        if k == 0:
+            send_ids()
     for c in loads:
         c.wait()
 
@@ -319,17 +330,26 @@
     def begin(stream):
         for k in stream.blocks:
             arrive(k)
+            if len(stream.blocks) == 1 and (k + 1) * BLK == 2 * stream.H and stream.H % BLK == 0:
+                stream.strip_half(k, x, xw, 1 - core)
+                stream.at = 2 * stream.H
+                stream.pair_start()
+                stream.strip_half(k, x, xw, core)
+                return
             stream.strip(k, x, xw)
         stream.pair_start()
-        stream.one_start()
 
     s1, s2, s3, s4 = streams
     begin(s1)
+    s1.one_start()
     begin(s2)
+    s2.one_start()
     s1.two_start()
     begin(s3)
+    s3.one_start()
+    begin(s4)
     s2.two_start()
-    begin(s4)
+    s4.one_start()
 
     arrived(ids, i_r)
     owner = lax.div(b * kc, kl)
@@ -374,6 +394,10 @@
     s4.back_start()
     s1.spread_rest()
     s2.spread_rest()
+    arrived(x.at[:n_sent, :], x_s)
+    arrived(ids.at[:, :R - 1], i_s)
+    for stream in streams:
+        stream.settle()
     s3.pair_back()
     s1.pair_back()
     s2.pair_back()
@@ -381,20 +405,20 @@
     s4.pair_back()
     gather(s1)
     gather(s2)
+    for stream in streams[:-1]:
+        stream.finish()
     gather(s4)
     t = t_m[...] + t_o[...] * c_col
-    g_o = times_left(brow[:, :cut], t[:cut, :])
-    g_m = times_left(brow[:, cut:], t[cut:, :])
-    gram_ref[...] = g_m + g_o * jnp.concatenate([c_row] * (kc // 128), axis=1)
-    arrived(x.at[:n_sent, :], x_s)
-    arrived(ids.at[:, :R - 1], i_s)
-    for stream in streams:
-        stream.finish()
-
-
-def times_left(s, v):
-    a, b = split(v)
-    return dot(s, a) + dot(s, b)
+    t_hi, t_lo = split(t)
+    step = kl // 4
+    for at in range(0, kl, step):
+        rows = slice(at, at + step)
+        g_o = dot(brow[rows, :cut], t_hi[:cut, :]) + dot(brow[rows, :cut], t_lo[:cut, :])
+        g_m = dot(brow[rows, cut:], t_hi[cut:, :]) + dot(brow[rows, cut:], t_lo[cut:, :])
+        gram[rows, :] = g_m + g_o * jnp.concatenate([c_row[rows, :]] * (kc // 128), axis=1)
+        pltpu.make_async_copy(gram.at[rows, :], gram_ref.at[rows, :], g_s).start()
+    arrived(gram, g_s)
+    s4.finish()
 
 
 def plan(nblk):
@@ -450,7 +474,6 @@
         nblk = n // BLK
         kl = mon_id.shape[0]
         kc = kl * R // B
-        vmem = pl.BlockSpec(memory_space=pltpu.VMEM)
         hbm = pl.BlockSpec(memory_space=pl.ANY)
         dma = pltpu.SemaphoreType.DMA
         streams = plan(nblk)
@@ -458,7 +481,7 @@
             functools.partial(kernel, (R, B, cols * B)),
             out_shape=jax.ShapeDtypeStruct((kl, kc), F32),
             in_specs=[hbm] * 7,
-            out_specs=vmem,
+            out_specs=hbm,
             scratch_shapes=[
                 pltpu.VMEM((1, cols), F32),
                 pltpu.VMEM((1, lodf_table.shape[0]), F32),
@@ -473,7 +496,7 @@
                 pltpu.VMEM((kl, n), BF16),
                 pltpu.VMEM((n, kc), F32),
                 pltpu.VMEM((n, kc), F32),
-                dma, dma((nblk,)), dma, dma,
+                dma, dma((nblk,)), dma, dma, pltpu.VMEM((kl, kc), F32), dma,
             ] + [
                 ref for blocks, direct in streams
                 for ref in (direct_scratch(sum(k + 1 for k in blocks)) if direct else

time: 43.8 us -> 43.1 us (0.984)
  Pallas kernels: 41.8 us -> 41 us
    pallas_call x1, Pallas kernels: 41.8 us -> 41 us  [local(): pl.pallas_call(functools.partial(kernel, (R, B, cols * B)), out_shape=jax...]
where the time goes in v3:
time: 43.1 us; the launch traced here: 42.9 us
  Pallas kernels  41 us (95%)
  local copies, waits for them, and re-layouts  1.87 us (4%)
    pallas_call x1, Pallas kernels, local(): pl.pallas_call(functools.partial(kernel, (R, B, cols * B)), out_shape=jax...  41 us
    unnamed x1, local copies, waits for them, and re-layouts  1.87 us

profile of v3, /device:TPU:1, one launch (start us, length us, event | category | flops | bytes accessed | tf_op | source)
XLA Modules:
  0.0 42.9 jit_solution(17823590848058212207)
XLA Ops:
  0.0 41.0 %shard_map.73 = f32[512,256]{1,0:T(8,128)} custom-call(bf16[128,4096]{1,0:T(8,128)(2,1)} %mon_ref.1, bf16[64,4096]{1,0:T(8,128)(2,1)} %out_ref.1, f32[1,4096]{1,0:T(1,128)} %bitcast.5, f32[1,1024]{1,0:T(1,128)} %bitcast.6, s32[1,512]{1,0:T(1,128)} %bitcast.7, s32[1,512]{1,0:T(1,128)} %bitcast.8, s32[1,512]{1,0:T(1,128)} %bitcast.9), custom_call_target="tpu_custom_call" | custom-call | tf_op jit(solution)/shard_map/pallas_call | solution.py:480
  41.1 1.9 %copy.9 = f32[512,256]{1,0:T(8,128)} copy(f32[512,256]{1,0:T(8,128)} %shard_map.73) | data formatting | bytes 1048576

commit v4 on v3

--- a/solution.py
+++ b/solution.py
@@ -1,4 +1,5 @@
 import functools
+import math
 
 import jax
 import jax.numpy as jnp
@@ -8,6 +9,7 @@
 from jax.sharding import PartitionSpec as P
 
 BLK = 128
+TINY = 1e-30
 BOUND = 6.0 * 6.0 * 4.0 * 1.01
 F32 = jnp.float32
 BF16 = jnp.bfloat16
@@ -30,11 +32,9 @@
 
 
 def encode(v, bound):
-    u = jnp.abs(v) * (1.0 / bound)
-    for _ in range(4):
-        u = jnp.sqrt(u)
-    u = jnp.minimum(u * 32767.0 + 0.5, 32767.0)
-    return jnp.where(v < 0, -u, u).astype(jnp.int32).astype(jnp.int16)
+    u = jnp.log2(jnp.maximum(jnp.abs(v), TINY)) * (1 / 16) + math.log2(32767.0 / bound ** (1 / 16))
+    u = jnp.minimum(jnp.exp2(u) + 0.5, 32767.0)
+    return jnp.where(v < 0, -u, u).astype(jnp.int32).astype(I16)
 
 
 def decode(q, bound):

time: 43.1 us -> 42.7 us (level)
  no operation moved by 1% of the time
where the time goes in v4:
time: 42.7 us; the launch traced here: 42.6 us
  Pallas kernels  40.7 us (95%)
  local copies, waits for them, and re-layouts  1.87 us (4%)
    pallas_call x1, Pallas kernels, local(): pl.pallas_call(functools.partial(kernel, (R, B, cols * B)), out_shape=jax...  40.7 us
    unnamed x1, local copies, waits for them, and re-layouts  1.87 us

profile of v4, /device:TPU:1, one launch (start us, length us, event | category | flops | bytes accessed | tf_op | source)
XLA Modules:
  0.0 42.6 jit_solution(15528951168372903673)
XLA Ops:
  0.0 40.7 %shard_map.73 = f32[512,256]{1,0:T(8,128)} custom-call(bf16[128,4096]{1,0:T(8,128)(2,1)} %mon_ref.1, bf16[64,4096]{1,0:T(8,128)(2,1)} %out_ref.1, f32[1,4096]{1,0:T(1,128)} %bitcast.5, f32[1,1024]{1,0:T(1,128)} %bitcast.6, s32[1,512]{1,0:T(1,128)} %bitcast.7, s32[1,512]{1,0:T(1,128)} %bitcast.8, s32[1,512]{1,0:T(1,128)} %bitcast.9), custom_call_target="tpu_custom_call" | custom-call | tf_op jit(solution)/shard_map/pallas_call | solution.py:480
  40.7 1.9 %copy.9 = f32[512,256]{1,0:T(8,128)} copy(f32[512,256]{1,0:T(8,128)} %shard_map.73) | data formatting | bytes 1048576

commit v5 on v4

--- a/solution.py
+++ b/solution.py
@@ -365,10 +365,8 @@
     cut = nblk_o * BLK
 
     def times(v, cols_of):
-        total = None
-        for p in split(v):
-            total = dot(p, cols_of) if total is None else total + dot(p, cols_of)
-        return total
+        a, b = split(v)
+        return dot(jnp.concatenate([a, b], axis=1), jnp.concatenate([cols_of, cols_of], axis=0))
 
     def gather(stream):
         at = 0

time: 42.7 us -> 42.3 us (level)
  no operation moved by 1% of the time
where the time goes in v5:
time: 42.3 us; the launch traced here: 42.2 us
  Pallas kernels  40.3 us (95%)
  local copies, waits for them, and re-layouts  1.87 us (4%)
    pallas_call x1, Pallas kernels, local(): pl.pallas_call(functools.partial(kernel, (R, B, cols * B)), out_shape=jax...  40.3 us
    unnamed x1, local copies, waits for them, and re-layouts  1.87 us

profile of v5, /device:TPU:1, one launch (start us, length us, event | category | flops | bytes accessed | tf_op | source)
XLA Modules:
  0.0 42.2 jit_solution(7243414129410324405)
XLA Ops:
  0.0 40.3 %shard_map.73 = f32[512,256]{1,0:T(8,128)} custom-call(bf16[128,4096]{1,0:T(8,128)(2,1)} %mon_ref.1, bf16[64,4096]{1,0:T(8,128)(2,1)} %out_ref.1, f32[1,4096]{1,0:T(1,128)} %bitcast.5, f32[1,1024]{1,0:T(1,128)} %bitcast.6, s32[1,512]{1,0:T(1,128)} %bitcast.7, s32[1,512]{1,0:T(1,128)} %bitcast.8, s32[1,512]{1,0:T(1,128)} %bitcast.9), custom_call_target="tpu_custom_call" | custom-call | tf_op jit(solution)/shard_map/pallas_call | solution.py:478
  40.3 1.9 %copy.9 = f32[512,256]{1,0:T(8,128)} copy(f32[512,256]{1,0:T(8,128)} %shard_map.73) | data formatting | bytes 1048576

commit v6 on v5

--- a/solution.py
+++ b/solution.py
@@ -237,7 +237,7 @@
 
 
 def kernel(dims, mon_ref, out_ref, w_hbm, table_hbm, mid_hbm, oid_hbm, lid_hbm,
-           gram_ref, w_ref, table_ref, mid_ref, oid_ref, lid_ref, small, x, xw, tt, ids, brow, t_o, t_m, x_s, x_r, i_s, i_r, gram, g_s, *rest):
+           gram_ref, w_ref, table_ref, small, x, xw, tt, ids, brow, t_o, t_m, x_s, x_r, i_s, i_r, gram, g_s, *rest):
     R, B, nb_all = dims
     Z = B // 2
     r = lax.axis_index("row")
@@ -251,7 +251,7 @@
     nblk_o, nblk_m = orows // each, mrows // each
     nblk = nblk_m + nblk_o
     n_sent = (R - 1) * (mrows + orows)
-    kl = mid_ref.shape[1]
+    kl = mid_hbm.shape[1]
     kc = kl * R // B
     def row_dev(q):
         return {"row": q}
@@ -267,8 +267,7 @@
         pl.semaphore_signal(barrier, inc=1, device_id=z_dev(lax.rem(zi + d, Z)), device_id_type=MESH)
     pl.semaphore_signal(barrier, inc=1, device_id=pair_dev, device_id_type=MESH)
     loads = []
-    for i, (src, dst) in enumerate(((w_hbm, w_ref), (table_hbm, table_ref), (mid_hbm, mid_ref),
-                                    (oid_hbm, oid_ref), (lid_hbm, lid_ref))):
+    for i, (src, dst) in enumerate(((w_hbm, w_ref), (table_hbm, table_ref))):
         c = pltpu.make_async_copy(src, dst, small.at[i])
         c.start()
         loads.append(c)
@@ -296,13 +295,14 @@
             send_ids()
     for c in loads:
         c.wait()
+    arrived(ids, i_r)
 
     entries = table_ref.shape[1]
     for e in range(0, entries, 128):
         tt[e:e + 128, :] = down(table_ref[:, e:e + 128])
-    c_row = down(factors(lid_ref[...], tt, entries))
-    oid_t = down(oid_ref[...].astype(F32)).astype(jnp.int32)
-    mid_t = down(mid_ref[...].astype(F32)).astype(jnp.int32)
+    c_row = down(factors(ids[2, r], tt, entries))
+    oid_t = down(ids[1, r].astype(F32)).astype(jnp.int32)
+    mid_t = down(ids[0, r].astype(F32)).astype(jnp.int32)
     for k in range(nblk):
         for e in range(0, BLK, 128):
             at = slice(k * BLK + e, k * BLK + e + 128)
@@ -342,6 +342,14 @@
     s1, s2, s3, s4 = streams
     begin(s1)
     s1.one_start()
+    owner = lax.div(b * kc, kl)
+    start = pl.multiple_of(lax.rem(b * kc, kl), 128)
+    mid_c = ids[0, owner, :, pl.ds(start, kc)]
+    oid_c = ids[1, owner, :, pl.ds(start, kc)]
+    c_col = factors(ids[2, owner, :, pl.ds(start, kc)], tt, entries)
+    bcol = [select(oid_c, (k, 0), each, orows, 0, (BLK, kc)) for k in range(nblk_o)]
+    bcol += [select(mid_c, (k, 0), each, mrows, 0, (BLK, kc)) for k in range(nblk_m)]
+
     begin(s2)
     s2.one_start()
     s1.two_start()
@@ -350,15 +358,6 @@
     begin(s4)
     s2.two_start()
     s4.one_start()
-
-    arrived(ids, i_r)
-    owner = lax.div(b * kc, kl)
-    begin = pl.multiple_of(lax.rem(b * kc, kl), 128)
-    mid_c = ids[0, owner, :, pl.ds(begin, kc)]
-    oid_c = ids[1, owner, :, pl.ds(begin, kc)]
-    c_col = factors(ids[2, owner, :, pl.ds(begin, kc)], tt, entries)
-    bcol = [select(oid_c, (k, 0), each, orows, 0, (BLK, kc)) for k in range(nblk_o)]
-    bcol += [select(mid_c, (k, 0), each, mrows, 0, (BLK, kc)) for k in range(nblk_m)]
 
     t_o[...] = jnp.zeros_like(t_o)
     t_m[...] = jnp.zeros_like(t_m)
@@ -483,10 +482,7 @@
             scratch_shapes=[
                 pltpu.VMEM((1, cols), F32),
                 pltpu.VMEM((1, lodf_table.shape[0]), F32),
-                pltpu.VMEM((1, kl), jnp.int32),
-                pltpu.VMEM((1, kl), jnp.int32),
-                pltpu.VMEM((1, kl), jnp.int32),
-                dma((5,)),
+                dma((2,)),
                 pltpu.VMEM((n, cq), BF16),
                 pltpu.VMEM((nblk, 2 * BLK, cq), BF16),
                 pltpu.VMEM((lodf_table.shape[0], 128), F32),

time: 42.3 us -> 42.3 us (level)
  no operation moved by 1% of the time
where the time goes in v6:
time: 42.3 us; the launch traced here: 42.1 us
  Pallas kernels  40.3 us (95%)
  local copies, waits for them, and re-layouts  1.87 us (4%)
    pallas_call x1, Pallas kernels, local(): pl.pallas_call(functools.partial(kernel, (R, B, cols * B)), out_shape=jax...  40.3 us
    unnamed x1, local copies, waits for them, and re-layouts  1.87 us

profile of v6, /device:TPU:1, one launch (start us, length us, event | category | flops | bytes accessed | tf_op | source)
XLA Modules:
  0.0 42.1 jit_solution(167209552769610771)
XLA Ops:
  0.0 40.3 %shard_map.73 = f32[512,256]{1,0:T(8,128)} custom-call(bf16[128,4096]{1,0:T(8,128)(2,1)} %mon_ref.1, bf16[64,4096]{1,0:T(8,128)(2,1)} %out_ref.1, f32[1,4096]{1,0:T(1,128)} %bitcast.5, f32[1,1024]{1,0:T(1,128)} %bitcast.6, s32[1,512]{1,0:T(1,128)} %bitcast.7, s32[1,512]{1,0:T(1,128)} %bitcast.8, s32[1,512]{1,0:T(1,128)} %bitcast.9), custom_call_target="tpu_custom_call" | custom-call | tf_op jit(solution)/shard_map/pallas_call | solution.py:477
  40.3 1.9 %copy.9 = f32[512,256]{1,0:T(8,128)} copy(f32[512,256]{1,0:T(8,128)} %shard_map.73) | data formatting | bytes 1048576
